TPU v7x, 512 devices: a whole 4x8x8 slice. The times are simulated.
512 devices in a mesh: row: 8 (over z_lo, core), bulk: 64 (over z_hi, x, y).
Axes of the slice: x: 4, y: 8, z: 8 (z_hi: 2, z_lo: 4; z = z_hi * 4 + z_lo), core: 2. Of those that a mesh axis runs over, the one named last changes fastest.
Arguments:
- residual_in: float32 [2048, 65536], P('row', 'bulk'), may hold values from -6 to 6
- amplitudes: float32 [2048, 2048], P('row', 'bulk'), may hold values from -6 to 6
- integral_tiles: float32 [4096, 128, 128], P('bulk', 'row'), may hold values from -0.1875 to 0.1875
- tile_reader: int32 [4096, 1], P('bulk'), may hold values from 0 to 63; in each aligned block of 64 rows (0 to 63, 64 to 127, ...) at most 2 rows name the same one
- tile_k: int32 [4096], P('bulk'), may hold values from 0 to 15
- tile_column: int32 [4096], P('bulk'), may hold values from 0 to 7
Outputs:
- residual_out: float32 [2048, 65536], P('row', 'bulk')
Inputs may be any that keep to these rules, and one draw needn't show every extreme that they name: `tile_reader`: among the 64 tiles stored on one index of bulk (aligned blocks of 64 entries), at most 2 name the same reader; some block has exactly 2 for some reader.
All inputs are finite; a program needn't handle non-finite values.
Results may differ from a plain program's by a relative error of at most 0.0003.
Values sent between devices are 32-bit elements; how exact they have to be, the bound alone decides.
A program may use at most 64 MiB of HBM per device.

v0:
```python
import jax
import jax.numpy as jnp
import numpy as np
from jax import lax
from jax.sharding import Mesh, PartitionSpec as P

KT = 16
CT = 8
SLOT = 2


def bucket_slots(tile_reader, tile_k, tile_column, targets, slots):
    readers = tile_reader[:, 0]
    matches = (readers[:, None] == jnp.arange(targets, dtype=jnp.int32)[None, :]).astype(jnp.int32)
    ordinal = jnp.cumsum(matches, axis=0) - matches
    position = jnp.sum(ordinal * matches, axis=1)
    select = matches.T[:, None, :] * (
        position[None, None, :] == jnp.arange(slots, dtype=jnp.int32)[None, :, None]
    ).astype(jnp.int32)
    filled = jnp.sum(select, axis=2)
    local_index = jnp.sum(
        select * jnp.arange(readers.shape[0], dtype=jnp.int32)[None, None, :], axis=2
    )
    slot_tile = jnp.sum(select * tile_k[None, None, :], axis=2) + filled - 1
    slot_column = jnp.sum(select * tile_column[None, None, :], axis=2) + filled - 1
    return (filled, local_index, slot_tile, slot_column)


def local(residual_in, amplitudes, integral_tiles, tile_reader, tile_k, tile_column):
    targets = lax.axis_size("bulk")
    height, width = (integral_tiles.shape[1], integral_tiles.shape[2])
    filled, local_index, slot_tile, slot_column = bucket_slots(
        tile_reader, tile_k, tile_column, targets, SLOT
    )
    picked = jnp.take(integral_tiles, local_index.reshape(-1), axis=0)
    picked = jnp.where(filled.reshape(-1)[:, None, None] > 0, picked, 0.0)
    outgoing = picked.reshape(targets, SLOT, height, width)
    arrived, arrived_tile, arrived_column = (
        lax.all_to_all(outgoing, "bulk", split_axis=0, concat_axis=0, tiled=True),
        lax.all_to_all(slot_tile, "bulk", split_axis=0, concat_axis=0, tiled=True),
        lax.all_to_all(slot_column, "bulk", split_axis=0, concat_axis=0, tiled=True),
    )
    arrived = arrived.reshape(targets * SLOT, height * width)
    position = arrived_tile.reshape(-1) * CT + arrived_column.reshape(-1)
    table = (position[None, :] == jnp.arange(KT * CT, dtype=jnp.int32)[:, None]).astype(jnp.float32)
    placed = jnp.dot(table, arrived, precision=lax.Precision.HIGHEST)
    placed = (
        placed.reshape(KT, CT, height, width).transpose(0, 2, 1, 3).reshape(KT * height, CT * width)
    )
    gathered = lax.all_gather(placed, "zl", axis=0, tiled=False)
    gathered = lax.all_gather(gathered, "core", axis=1, tiled=False)
    dense = gathered.reshape(-1, CT * width)
    amps = lax.all_gather(amplitudes, "bulk", axis=1, tiled=True)
    rows = amps.shape[0]
    groups = gathered.shape[0] * gathered.shape[1]
    amps = amps.reshape(rows, KT, groups, height).transpose(0, 2, 1, 3).reshape(rows, -1)
    return residual_in + jnp.dot(amps, dense, precision=lax.Precision.HIGHEST)


def solution(mesh):
    row_size = mesh.shape["row"]
    devices = np.asarray(mesh.devices).reshape(row_size // 2, 2, mesh.shape["bulk"])
    inner = Mesh(devices, ("zl", "core", "bulk"))
    row = ("zl", "core")
    placed = (
        P(row, "bulk"),
        P(row, "bulk"),
        P("bulk", row, None),
        P("bulk", None),
        P("bulk"),
        P("bulk"),
    )
    return jax.shard_map(
        local, mesh=inner, in_specs=placed, out_specs=P(row, "bulk"), check_vma=False
    )
```

profile of v0, /device:TPU:1, one launch (start us, length us, event | category | flops | bytes accessed | tf_op | source)
XLA Modules:
  0.0 376.1 jit_solution(10225368570562144597)
XLA Ops:
  6.5 0.8 fusion.9
  7.4 0.8 select_reduce_fusion
  8.3 0.9 fusion.1
  9.2 0.7 copy.34
  9.9 19.6 %all-to-all-start = ((s32[64,1,2]{2,1,0:T(1,128)}), s32[64,1,2]{2,1,0:T(1,128)S(1)}, u32[]{:S(2)}, u32[]{:S(2)}) async-start(s32[64,1,2]{2,1,0:T(1,128)} %copy.34), calls=%async_computation | async-start | bytes 65536 | tf_op jit(solution)/shard_map/all_to_all | solution.py:40
  29.5 0.1 copy.38
  29.6 0.1 reshape.184
  29.8 0.7 copy.35
  30.5 0.1 copy.36
  30.6 0.1 copy.37
  30.7 0.8 gather_fusion
  31.5 11.1 %all-to-all-done = s32[64,1,2]{2,1,0:T(1,128)S(1)} async-done(((s32[64,1,2]{2,1,0:T(1,128)}), s32[64,1,2]{2,1,0:T(1,128)S(1)}, u32[]{:S(2)}, u32[]{:S(2)}) %all-to-all-start) | async-done | bytes 544 | tf_op jit(solution)/shard_map/all_to_all | solution.py:40
  42.6 4.5 %all-to-all-start.1 = ((s32[64,1,2]{2,1,0:T(1,128)}), s32[64,1,2]{2,1,0:T(1,128)S(1)}, u32[]{:S(2)}, u32[]{:S(2)}) async-start(s32[64,1,2]{2,1,0:T(1,128)} %copy.35), calls=%async_computation.1 | async-start | bytes 65536 | tf_op jit(solution)/shard_map/all_to_all | solution.py:41
  47.2 1.3 select_select_fusion
  48.5 11.9 %all-to-all-done.1 = s32[64,1,2]{2,1,0:T(1,128)S(1)} async-done(((s32[64,1,2]{2,1,0:T(1,128)}), s32[64,1,2]{2,1,0:T(1,128)S(1)}, u32[]{:S(2)}, u32[]{:S(2)}) %all-to-all-start.1) | async-done | bytes 544 | tf_op jit(solution)/shard_map/all_to_all | solution.py:41
  60.4 4.7 %all-to-all-start.2 = ((f32[64,2,16,128]{3,2,1,0:T(8,128)}), f32[64,2,16,128]{3,2,1,0:T(8,128)S(1)}, u32[]{:S(2)}, u32[]{:S(2)}) async-start(f32[64,2,16,128]{3,2,1,0:T(8,128)} %select_select_fusion), calls=%async_computation.2 | async-start | bytes 2097152 | tf_op jit(solution)/shard_map/all_to_all | solution.py:39
  65.1 0.1 add_reduce_fusion
  65.2 0.1 add.82
  65.4 28.7 %all-to-all-done.2 = f32[64,2,16,128]{3,2,1,0:T(8,128)S(1)} async-done(((f32[64,2,16,128]{3,2,1,0:T(8,128)}), f32[64,2,16,128]{3,2,1,0:T(8,128)S(1)}, u32[]{:S(2)}, u32[]{:S(2)}) %all-to-all-start.2) | async-done | bytes 1048608 | tf_op jit(solution)/shard_map/all_to_all | solution.py:39
  94.0 0.3 copy.46
  94.4 0.3 copy.39
  94.7 0.7 convolution_bitcast_fusion.1
  95.4 1.1 all_gather_reshape.3
  96.6 0.7 all-gather.7.cloned.1.call-update
  97.3 0.2 all-gather.9.cloned.1.call-start
  97.6 84.4 %all-gather.5.cloned.1.call-done = f32[4,256,1024]{2,1,0:T(8,128)} async-done(((f32[1,256,1024]{2,1,0:T(8,128)}), f32[4,256,1024]{2,1,0:T(8,128)}) %all-gather.5.cloned.1.call-update) | async-done | bytes 4194320 | tf_op jit(solution)/shard_map/all_gather | solution.py:50
  182.0 1.3 copy.41
  183.3 138.8 %all-gather.7.cloned.1.call-done = f32[256,2048]{0,1:T(8,128)} async-done(((f32[256,32]{0,1:T(8,128)}), f32[256,2048]{0,1:T(8,128)}) %all-gather.7.cloned.1.call-update) | async-done | bytes 2097168 | tf_op jit(solution)/shard_map/all_gather | solution.py:53
  322.1 1.8 copy.40
  324.0 26.6 %all-gather.9.cloned.1.call-done = f32[4,512,1024]{2,1,0:T(8,128)} async-done(((f32[4,256,1024]{2,1,0:T(8,128)}), f32[4,512,1024]{2,1,0:T(8,128)}) %all-gather.9.cloned.1.call-update) | async-done | bytes 8388624 | tf_op jit(solution)/shard_map/all_gather | solution.py:51
  350.6 16.5 %fusion = f32[256,1024]{0,1:T(8,128)} fusion(f32[256,1024]{0,1:T(8,128)} %copy.41, f32[2048,1024]{1,0:T(8,128)} %bitcast.40, f32[256,2048]{0,1:T(8,128)S(1)} %bitcast.41), kind=kOutput, calls=%fused_computation.3 | convolution fusion | flops 6442713088 | bytes 12582912 | tf_op jit(solution)/shard_map/dot_general | solution.py:57
  367.1 2.5 copy.42
  (15 shorter events, 0.3 us)
Async XLA Ops:
  6.5 24.2 %copy-start = (f32[64,16,128]{2,1,0:T(8,128)S(1)}, f32[64,16,128]{2,1,0:T(8,128)}, u32[]{:S(2)}) copy-start(f32[64,16,128]{2,1,0:T(8,128)} %param.8) | copy-start | bytes 1572868
  9.9 32.7 %all-to-all-start = ((s32[64,1,2]{2,1,0:T(1,128)}), s32[64,1,2]{2,1,0:T(1,128)S(1)}, u32[]{:S(2)}, u32[]{:S(2)}) async-start(s32[64,1,2]{2,1,0:T(1,128)} %copy.34), calls=%async_computation | async-start | bytes 65536 | tf_op jit(solution)/shard_map/all_to_all | solution.py:40
  42.6 17.8 %all-to-all-start.1 = ((s32[64,1,2]{2,1,0:T(1,128)}), s32[64,1,2]{2,1,0:T(1,128)S(1)}, u32[]{:S(2)}, u32[]{:S(2)}) async-start(s32[64,1,2]{2,1,0:T(1,128)} %copy.35), calls=%async_computation.1 | async-start | bytes 65536 | tf_op jit(solution)/shard_map/all_to_all | solution.py:41
  60.4 33.6 %all-to-all-start.2 = ((f32[64,2,16,128]{3,2,1,0:T(8,128)}), f32[64,2,16,128]{3,2,1,0:T(8,128)S(1)}, u32[]{:S(2)}, u32[]{:S(2)}) async-start(f32[64,2,16,128]{3,2,1,0:T(8,128)} %select_select_fusion), calls=%async_computation.2 | async-start | bytes 2097152 | tf_op jit(solution)/shard_map/all_to_all | solution.py:39
  65.0 116.9 %all-gather.5.cloned.1.call-start = ((), (), s32[]{:S(2)}) async-start(), calls=%async_computation.3 | async-start | bytes 5242880 | tf_op jit(solution)/shard_map/all_gather | solution.py:50
  95.4 86.6 %copy-start.1 = (f32[256,1024]{1,0:T(8,128)S(1)}, f32[256,1024]{1,0:T(8,128)}, u32[]{:S(2)}) copy-start(f32[256,1024]{1,0:T(8,128)} %param.6) | copy-start | bytes 3145732
  96.6 225.6 %all-gather.7.cloned.1.call-start = ((), (), s32[]{:S(2)}) async-start(), calls=%async_computation.4 | async-start | bytes 2129920 | tf_op jit(solution)/shard_map/all_gather | solution.py:53
  97.3 253.2 %all-gather.9.cloned.1.call-start = ((), (), s32[]{:S(2)}) async-start(), calls=%async_computation.5 | async-start | bytes 12582912 | tf_op jit(solution)/shard_map/all_gather | solution.py:51
Sparse Core Ops, SparseCore 0:
  96.7 85.2 all-gather.4
  186.5 135.6 all-gather.6
  324.2 26.2 all-gather.8
where the time goes:
time: 377 us; the launch traced here: 376 us
  waiting for transfers between devices  302 us (80%)
  starting transfers between devices  29.1 us (8%)
  matrix products  17.2 us (5%)
  between operations  13.3 us (4%)
  local copies, waits for them, and re-layouts  10.2 us (3%)
  other arithmetic  4.08 us (1%)
    all_gather x1, waiting for transfers between devices, local(): amps = lax.all_gather(amplitudes, 'bulk', axis=1, tiled=True)  139 us
    all_gather x1, waiting for transfers between devices, local(): gathered = lax.all_gather(placed, 'zl', axis=0, tiled=False)  84.4 us
    all_to_all x1, waiting for transfers between devices, local(): lax.all_to_all(outgoing, 'bulk', split_axis=0, concat_axis=0, tiled=True)  28.7 us
    all_gather x1, waiting for transfers between devices, local(): gathered = lax.all_gather(gathered, 'core', axis=1, tiled=False)  26.6 us
    all_to_all x1, starting transfers between devices, local(): lax.all_to_all(slot_tile, 'bulk', split_axis=0, concat_axis=0, tiled=True)  19.6 us
    dot_general x1, matrix products, local(): return residual_in + jnp.dot(amps, dense, precision=lax.Precision.HIGHEST)  16.5 us
    all_to_all x1, waiting for transfers between devices, local(): lax.all_to_all(slot_column, 'bulk', split_axis=0, concat_axis=0, tiled=True)  11.9 us
    all_to_all x1, waiting for transfers between devices, local(): lax.all_to_all(slot_tile, 'bulk', split_axis=0, concat_axis=0, tiled=True)  11.1 us
  transfers between devices with their start and end apart: 6, of which 6 were waited for; matrix products, arithmetic and copies ran while one was open for 2% of the time, Pallas kernels for 0%

commit v1 on v0

--- a/solution.py
+++ b/solution.py
@@ -50,7 +50,9 @@
     gathered = lax.all_gather(placed, "zl", axis=0, tiled=False)
     gathered = lax.all_gather(gathered, "core", axis=1, tiled=False)
     dense = gathered.reshape(-1, CT * width)
-    amps = lax.all_gather(amplitudes, "bulk", axis=1, tiled=True)
+    amps = jnp.concatenate(
+        lax.all_to_all(jnp.stack([amplitudes] * lax.axis_size("bulk")), "bulk", 0, 0), axis=1
+    )
     rows = amps.shape[0]
     groups = gathered.shape[0] * gathered.shape[1]
     amps = amps.reshape(rows, KT, groups, height).transpose(0, 2, 1, 3).reshape(rows, -1)

time: 377 us -> 283 us (0.75)
  waiting for transfers between devices: 302 us -> 188 us
  starting transfers between devices: 29.1 us -> 43.5 us
  local copies, waits for them, and re-layouts: 10.2 us -> 15.3 us
    all_gather x1 -> x0, waiting for transfers between devices: 139 us -> none  [local(): amps = lax.all_gather(amplitudes, 'bulk', axis=1, tiled=True)]
    all_to_all x0 -> x1, waiting for transfers between devices: none -> 50.7 us  [local(): lax.all_to_all(jnp.stack([amplitudes] * lax.axis_size('bulk')), 'bulk', 0...]
    all_gather x1, waiting for transfers between devices: 26.6 us -> 0.02 us  [local(): gathered = lax.all_gather(gathered, 'core', axis=1, tiled=False)]
    all_to_all x0 -> x1, starting transfers between devices: none -> 14.7 us  [local(): lax.all_to_all(jnp.stack([amplitudes] * lax.axis_size('bulk')), 'bulk', 0...]
  transfers between devices with their start and end apart: 6 -> 6, of which waited for: 6 -> 5; matrix products, arithmetic and copies ran while one was open for 2% -> 3% of each run, Pallas kernels for 0% -> 0%
where the time goes in v1:
time: 283 us; the launch traced here: 282 us
  waiting for transfers between devices  188 us (66%)
  starting transfers between devices  43.5 us (15%)
  matrix products  17.2 us (6%)
  local copies, waits for them, and re-layouts  15.3 us (5%)
  between operations  13.6 us (5%)
  other arithmetic  4.08 us (1%)
    all_gather x1, waiting for transfers between devices, local(): gathered = lax.all_gather(placed, 'zl', axis=0, tiled=False)  85.3 us
    all_to_all x1, waiting for transfers between devices, local(): lax.all_to_all(jnp.stack([amplitudes] * lax.axis_size('bulk')), 'bulk', 0...  50.7 us
    all_to_all x1, waiting for transfers between devices, local(): lax.all_to_all(outgoing, 'bulk', split_axis=0, concat_axis=0, tiled=True)  28.7 us
    all_to_all x1, starting transfers between devices, local(): lax.all_to_all(slot_tile, 'bulk', split_axis=0, concat_axis=0, tiled=True)  19.6 us
    dot_general x1, matrix products, local(): return residual_in + jnp.dot(amps, dense, precision=lax.Precision.HIGHEST)  16.5 us
    all_to_all x1, starting transfers between devices, local(): lax.all_to_all(jnp.stack([amplitudes] * lax.axis_size('bulk')), 'bulk', 0...  14.7 us
    all_to_all x1, waiting for transfers between devices, local(): lax.all_to_all(slot_column, 'bulk', split_axis=0, concat_axis=0, tiled=True)  11.9 us
    all_to_all x1, waiting for transfers between devices, local(): lax.all_to_all(slot_tile, 'bulk', split_axis=0, concat_axis=0, tiled=True)  11.1 us
  transfers between devices with their start and end apart: 6, of which 5 were waited for; matrix products, arithmetic and copies ran while one was open for 3% of the time, Pallas kernels for 0%

profile of v1, /device:TPU:1, one launch (start us, length us, event | category | flops | bytes accessed | tf_op | source)
XLA Modules:
  0.0 281.5 jit_solution(14336092096046881125)
XLA Ops:
  6.5 0.8 fusion.9
  7.4 0.8 select_reduce_fusion
  8.3 0.9 fusion.1
  9.2 0.7 copy.29
  9.9 19.6 %all-to-all-start = ((s32[64,1,2]{2,1,0:T(1,128)}), s32[64,1,2]{2,1,0:T(1,128)S(1)}, u32[]{:S(2)}, u32[]{:S(2)}) async-start(s32[64,1,2]{2,1,0:T(1,128)} %copy.29), calls=%async_computation | async-start | bytes 65536 | tf_op jit(solution)/shard_map/all_to_all | solution.py:40
  29.6 0.1 reshape.186
  29.8 0.7 copy.30
  30.5 0.1 copy.31
  30.6 0.1 copy.32
  30.7 0.8 gather_fusion
  31.5 11.1 %all-to-all-done = s32[64,1,2]{2,1,0:T(1,128)S(1)} async-done(((s32[64,1,2]{2,1,0:T(1,128)}), s32[64,1,2]{2,1,0:T(1,128)S(1)}, u32[]{:S(2)}, u32[]{:S(2)}) %all-to-all-start) | async-done | bytes 544 | tf_op jit(solution)/shard_map/all_to_all | solution.py:40
  42.6 4.5 %all-to-all-start.1 = ((s32[64,1,2]{2,1,0:T(1,128)}), s32[64,1,2]{2,1,0:T(1,128)S(1)}, u32[]{:S(2)}, u32[]{:S(2)}) async-start(s32[64,1,2]{2,1,0:T(1,128)} %copy.30), calls=%async_computation.1 | async-start | bytes 65536 | tf_op jit(solution)/shard_map/all_to_all | solution.py:41
  47.2 1.3 select_select_fusion
  48.5 11.9 %all-to-all-done.1 = s32[64,1,2]{2,1,0:T(1,128)S(1)} async-done(((s32[64,1,2]{2,1,0:T(1,128)}), s32[64,1,2]{2,1,0:T(1,128)S(1)}, u32[]{:S(2)}, u32[]{:S(2)}) %all-to-all-start.1) | async-done | bytes 544 | tf_op jit(solution)/shard_map/all_to_all | solution.py:41
  60.4 4.7 %all-to-all-start.2 = ((f32[64,2,16,128]{3,2,1,0:T(8,128)}), f32[64,2,16,128]{3,2,1,0:T(8,128)S(1)}, u32[]{:S(2)}, u32[]{:S(2)}) async-start(f32[64,2,16,128]{3,2,1,0:T(8,128)} %select_select_fusion), calls=%async_computation.2 | async-start | bytes 2097152 | tf_op jit(solution)/shard_map/all_to_all | solution.py:39
  65.1 0.1 add_reduce_fusion
  65.2 0.1 add.82
  65.4 28.7 %all-to-all-done.2 = f32[64,2,16,128]{3,2,1,0:T(8,128)S(1)} async-done(((f32[64,2,16,128]{3,2,1,0:T(8,128)}), f32[64,2,16,128]{3,2,1,0:T(8,128)S(1)}, u32[]{:S(2)}, u32[]{:S(2)}) %all-to-all-start.2) | async-done | bytes 1048608 | tf_op jit(solution)/shard_map/all_to_all | solution.py:39
  94.0 0.3 copy.41
  94.4 0.3 copy.34
  94.7 0.7 convolution_bitcast_fusion.1
  95.4 1.1 all_gather_reshape.3
  96.6 85.3 %all-gather.4.cloned.1.call-done = f32[4,256,1024]{2,1,0:T(8,128)} async-done(((f32[1,256,1024]{2,1,0:T(8,128)}), f32[4,256,1024]{2,1,0:T(8,128)}) %all-gather.4.cloned.1.call-update) | async-done | bytes 4194320 | tf_op jit(solution)/shard_map/all_gather | solution.py:50
  182.0 0.7 copy-done.2
  182.7 1.6 stack.2
  184.3 14.7 %all-to-all-start.3 = ((f32[64,256,32]{1,2,0:T(8,128)}), f32[64,256,32]{1,2,0:T(8,128)S(1)}, u32[]{:S(2)}, u32[]{:S(2)}) async-start(f32[64,256,32]{1,2,0:T(8,128)} %stack.2), calls=%async_computation.3 | async-start | bytes 4194304 | tf_op jit(solution)/shard_map/all_to_all | solution.py:54
  199.0 2.7 copy.36
  201.7 50.7 %all-to-all-done.3 = f32[64,256,32]{1,2,0:T(8,128)S(1)} async-done(((f32[64,256,32]{1,2,0:T(8,128)}), f32[64,256,32]{1,2,0:T(8,128)S(1)}, u32[]{:S(2)}, u32[]{:S(2)}) %all-to-all-start.3) | async-done | bytes 2097184 | tf_op jit(solution)/shard_map/all_to_all | solution.py:54
  252.5 1.3 copy-done.1
  253.8 1.8 copy.35
  255.7 16.5 %fusion = f32[256,1024]{0,1:T(8,128)} fusion(f32[256,1024]{0,1:T(8,128)} %copy.36, f32[2048,1024]{1,0:T(8,128)} %bitcast.42, f32[256,2048]{0,1:T(8,128)S(1)} %bitcast.43), kind=kOutput, calls=%fused_computation.3 | convolution fusion | flops 6442713088 | bytes 12582912 | tf_op jit(solution)/shard_map/dot_general | solution.py:59
  272.2 2.5 copy.37
  (17 shorter events, 0.4 us)
Async XLA Ops:
  6.5 24.2 %copy-start = (f32[64,16,128]{2,1,0:T(8,128)S(1)}, f32[64,16,128]{2,1,0:T(8,128)}, u32[]{:S(2)}) copy-start(f32[64,16,128]{2,1,0:T(8,128)} %param.8) | copy-start | bytes 1572868
  9.9 32.7 %all-to-all-start = ((s32[64,1,2]{2,1,0:T(1,128)}), s32[64,1,2]{2,1,0:T(1,128)S(1)}, u32[]{:S(2)}, u32[]{:S(2)}) async-start(s32[64,1,2]{2,1,0:T(1,128)} %copy.29), calls=%async_computation | async-start | bytes 65536 | tf_op jit(solution)/shard_map/all_to_all | solution.py:40
  42.6 17.8 %all-to-all-start.1 = ((s32[64,1,2]{2,1,0:T(1,128)}), s32[64,1,2]{2,1,0:T(1,128)S(1)}, u32[]{:S(2)}, u32[]{:S(2)}) async-start(s32[64,1,2]{2,1,0:T(1,128)} %copy.30), calls=%async_computation.1 | async-start | bytes 65536 | tf_op jit(solution)/shard_map/all_to_all | solution.py:41
  60.4 33.6 %all-to-all-start.2 = ((f32[64,2,16,128]{3,2,1,0:T(8,128)}), f32[64,2,16,128]{3,2,1,0:T(8,128)S(1)}, u32[]{:S(2)}, u32[]{:S(2)}) async-start(f32[64,2,16,128]{3,2,1,0:T(8,128)} %select_select_fusion), calls=%async_computation.2 | async-start | bytes 2097152 | tf_op jit(solution)/shard_map/all_to_all | solution.py:39
  65.0 116.9 %all-gather.4.cloned.1.call-start = ((), (), s32[]{:S(2)}) async-start(), calls=%async_computation.4 | async-start | bytes 5242880 | tf_op jit(solution)/shard_map/all_gather | solution.py:50
  96.6 159.1 %all-gather.6.cloned.1.call-start = ((), (), s32[]{:S(2)}) async-start(), calls=%async_computation.5 | async-start | bytes 12582912 | tf_op jit(solution)/shard_map/all_gather | solution.py:51
  181.9 0.8 copy-start.2
  184.3 68.2 %all-to-all-start.3 = ((f32[64,256,32]{1,2,0:T(8,128)}), f32[64,256,32]{1,2,0:T(8,128)S(1)}, u32[]{:S(2)}, u32[]{:S(2)}) async-start(f32[64,256,32]{1,2,0:T(8,128)} %stack.2), calls=%async_computation.3 | async-start | bytes 4194304 | tf_op jit(solution)/shard_map/all_to_all | solution.py:54
  252.5 1.3 copy-start.1
Sparse Core Ops, SparseCore 0:
  96.7 85.2 all-gather.3
  184.0 29.6 all-gather.5
